TPU v7x, 32 devices: a whole 2x2x4 slice. The times are simulated.
32 devices in a mesh: dp: 16 (over z, x, core), tensor: 2 (over y).
Axes of the slice: x: 2, y: 2, z: 4, core: 2. Of those that a mesh axis runs over, the one named last changes fastest.
Arguments:
- tokens: bfloat16 [1024, 16, 1152], P('tensor', 'dp'), may hold values from -6 to 6
- cond: bfloat16 [16, 1152], P('dp'), may hold values from -6 to 6
- mod_weight: bfloat16 [1152, 6912], P('dp'), may hold values from -0.1875 to 0.1875
- mod_bias: bfloat16 [6912], replicated, may hold values from -3 to 3
- query_key_value_weight: bfloat16 [1152, 3, 1152], P('dp', None, 'tensor'), may hold values from -0.1875 to 0.1875
- qkv_bias: bfloat16 [2, 1152], P(None, 'tensor'), may hold values from -3 to 3
- attention_out_weight: bfloat16 [1152, 1152], P('tensor', 'dp'), may hold values from -1.5 to 1.5
- attention_out_bias: bfloat16 [1152], replicated, may hold values from -3 to 3
- first_hidden_weight: bfloat16 [1152, 4608], P('dp', 'tensor'), may hold values from -0.1875 to 0.1875
- first_hidden_bias: bfloat16 [4608], P('tensor'), may hold values from -3 to 3
- second_hidden_weight: bfloat16 [4608, 1152], P('tensor', 'dp'), may hold values from -0.09375 to 0.09375
- second_hidden_bias: bfloat16 [1152], replicated, may hold values from -3 to 3
- out_grad: bfloat16 [1024, 16, 1152], P('tensor', 'dp'), may hold values from -6 to 6
Outputs:
- output: bfloat16 [1024, 16, 1152], P('tensor', 'dp')
- tokens_grad: bfloat16 [1024, 16, 1152], P('tensor', 'dp')
- cond_grad: float32 [16, 1152], P('dp')
- mod_weight_grad: float32 [1152, 6912], P('dp')
- mod_bias_grad: float32 [6912], replicated
- qkv_weight_grad: float32 [1152, 3, 1152], P('dp', None, 'tensor')
- qkv_bias_grad: float32 [2, 1152], P(None, 'tensor')
- proj_weight_grad: float32 [1152, 1152], P('tensor', 'dp')
- proj_bias_grad: float32 [1152], replicated
- fc1_weight_grad: float32 [1152, 4608], P('dp', 'tensor')
- fc1_bias_grad: float32 [4608], P('tensor')
- fc2_weight_grad: float32 [4608, 1152], P('tensor', 'dp')
- fc2_bias_grad: float32 [1152], replicated
All inputs are finite; a program needn't handle non-finite values.
Results may differ from a plain program's by a relative error of at most 0.02.
The roundings to bfloat16 on the way count: a program that leaves them out, or rounds other values in their place, can miss the bound.
Values may be sent and summed in bfloat16 or wider, within the bound.
A program may use at most 256 MiB of HBM per device.

v0:
```python
import jax
import jax.numpy as jnp
from jax import lax
from jax.sharding import PartitionSpec as P

HEADS = 16


def modulate(hidden, shifts, scales):
    center = hidden - jnp.mean(hidden, axis=-1, keepdims=True)
    spread = jnp.mean(center * center, axis=-1, keepdims=True)
    return center * lax.rsqrt(spread + 1e-06) * (1.0 + scales) + shifts


def gelu_tanh(values):
    return jax.nn.gelu(values, approximate=True)


def attend_forward(packed):
    queries = packed[:, 0]
    keys_all = packed[:, 1]
    values_all = packed[:, 2]
    seq_len = packed.shape[0]
    scaling = packed.shape[3] ** (-0.5)
    block_rows = min(512, seq_len)
    results = []
    log_parts = []
    for offset in range(0, seq_len, block_rows):
        query_block = queries[offset : offset + block_rows]
        scores = (
            jnp.einsum("qhe,khe->hqk", query_block, keys_all, preferred_element_type=jnp.float32)
            * scaling
        )
        highest = jnp.max(scores, axis=-1, keepdims=True)
        weights = jnp.exp(scores - highest)
        row_total = jnp.sum(weights, axis=-1, keepdims=True)
        prob_low = (weights / row_total).astype(jnp.bfloat16)
        mixture = jnp.einsum(
            "hqk,khe->qhe", prob_low, values_all, preferred_element_type=jnp.float32
        )
        results.append(mixture.reshape(block_rows, -1))
        log_parts.append((highest + jnp.log(row_total))[..., 0])
    return (jnp.concatenate(results, 0).astype(jnp.bfloat16), jnp.concatenate(log_parts, 1))


def attend_backward(inputs):
    packed, grad_out, log_totals = inputs
    queries = packed[:, 0]
    keys_all = packed[:, 1]
    values_all = packed[:, 2]
    seq_len = packed.shape[0]
    scaling = packed.shape[3] ** (-0.5)
    block_rows = min(512, seq_len)
    query_grads = []
    key_grad = jnp.zeros(keys_all.shape, jnp.float32)
    value_grad = jnp.zeros(values_all.shape, jnp.float32)
    for offset in range(0, seq_len, block_rows):
        query_block = queries[offset : offset + block_rows]
        grad_block = grad_out[offset : offset + block_rows]
        scores = (
            jnp.einsum("qhe,khe->hqk", query_block, keys_all, preferred_element_type=jnp.float32)
            * scaling
        )
        probs = jnp.exp(scores - log_totals[:, offset : offset + block_rows, None])
        prob_low = probs.astype(jnp.bfloat16)
        prob_grad = jnp.einsum(
            "qhe,khe->hqk", grad_block, values_all, preferred_element_type=jnp.float32
        )
        inner = jnp.sum(probs * prob_grad, axis=-1, keepdims=True)
        score_grad = (probs * (prob_grad - inner)).astype(jnp.bfloat16)
        query_grads.append(
            jnp.einsum("hqk,khe->qhe", score_grad, keys_all, preferred_element_type=jnp.float32)
            * scaling
        )
        key_grad = (
            key_grad
            + jnp.einsum(
                "hqk,qhe->khe", score_grad, query_block, preferred_element_type=jnp.float32
            )
            * scaling
        )
        value_grad = value_grad + jnp.einsum(
            "hqk,qhe->khe", prob_low, grad_block, preferred_element_type=jnp.float32
        )
    return jnp.stack([jnp.concatenate(query_grads, 0), key_grad, value_grad], 1).astype(
        jnp.bfloat16
    )


def on_device(
    tokens,
    cond,
    mod_weight,
    mod_bias,
    query_key_value_weight,
    qkv_bias,
    attention_out_weight,
    attention_out_bias,
    first_hidden_weight,
    first_hidden_bias,
    second_hidden_weight,
    second_hidden_bias,
    out_grad,
):
    w_mod, w_qkv, w_proj, w_fc1, w_fc2 = (
        lax.all_gather(mod_weight, "dp", axis=0, tiled=True),
        lax.all_gather(query_key_value_weight, "dp", axis=0, tiled=True),
        lax.all_gather(attention_out_weight, "dp", axis=1, tiled=True),
        lax.all_gather(first_hidden_weight, "dp", axis=0, tiled=True),
        lax.all_gather(second_hidden_weight, "dp", axis=1, tiled=True),
    )
    seq_local, latents, width = tokens.shape
    columns = query_key_value_weight.shape[2]
    head_size = width // HEADS
    heads_here = columns // head_size
    local_rows = seq_local * latents
    cond_wide = cond.astype(jnp.float32)
    silu_cond, silu_back = jax.vjp(jax.nn.silu, cond_wide)
    silu_low = silu_cond.astype(jnp.bfloat16)
    modulation = jnp.dot(silu_low, w_mod, preferred_element_type=jnp.float32) + mod_bias.astype(
        jnp.float32
    )
    pieces = modulation.reshape(latents, 6, width)
    hidden_in = tokens.astype(jnp.float32)
    attention_normalized, norm_a_back = jax.vjp(modulate, hidden_in, pieces[:, 0], pieces[:, 1])
    gathered_a = lax.all_gather(
        attention_normalized.astype(jnp.bfloat16), "tensor", axis=0, tiled=True
    )
    seq_len = gathered_a.shape[0]
    total_rows = seq_len * latents
    rows_a = gathered_a.reshape(total_rows, width)
    qkv_flat = w_qkv.reshape(width, 3 * columns)
    zero_row = jnp.zeros((columns,), jnp.float32)
    query_key_value_shift = jnp.stack(
        [qkv_bias[0].astype(jnp.float32), zero_row, qkv_bias[1].astype(jnp.float32)]
    )
    projected_output = (
        jnp.dot(rows_a, qkv_flat, preferred_element_type=jnp.float32).reshape(
            seq_len, latents, 3, columns
        )
        + query_key_value_shift
    )
    packed = jnp.moveaxis(projected_output.astype(jnp.bfloat16), 1, 0).reshape(
        latents, seq_len, 3, heads_here, head_size
    )
    attention_result, log_totals = lax.map(attend_forward, packed)
    attended_rows = jnp.moveaxis(attention_result, 0, 1).reshape(total_rows, columns)
    summed_a = lax.psum_scatter(
        jnp.dot(attended_rows, w_proj, preferred_element_type=jnp.float32).astype(jnp.bfloat16),
        "tensor",
        scatter_dimension=0,
        tiled=True,
    ).astype(jnp.float32)
    attention_branch = summed_a.reshape(seq_local, latents, width) + attention_out_bias.astype(
        jnp.float32
    )
    resid_mid = hidden_in + pieces[:, 2] * attention_branch
    feedforward_normalized, norm_m_back = jax.vjp(modulate, resid_mid, pieces[:, 3], pieces[:, 4])
    gathered_m = lax.all_gather(
        feedforward_normalized.astype(jnp.bfloat16), "tensor", axis=0, tiled=True
    )
    rows_m = gathered_m.reshape(total_rows, width)
    before_activation = jnp.dot(
        rows_m, w_fc1, preferred_element_type=jnp.float32
    ) + first_hidden_bias.astype(jnp.float32)
    gelu_activated, gelu_back = jax.vjp(gelu_tanh, before_activation)
    act_low = gelu_activated.astype(jnp.bfloat16)
    summed_m = lax.psum_scatter(
        jnp.dot(act_low, w_fc2, preferred_element_type=jnp.float32).astype(jnp.bfloat16),
        "tensor",
        scatter_dimension=0,
        tiled=True,
    ).astype(jnp.float32)
    feedforward_branch = summed_m.reshape(seq_local, latents, width) + second_hidden_bias.astype(
        jnp.float32
    )
    output = (resid_mid + pieces[:, 5] * feedforward_branch).astype(jnp.bfloat16)
    grad_out = out_grad.astype(jnp.float32)
    gate_m_grad = jnp.sum(grad_out * feedforward_branch, axis=0)
    grad_m_low = (grad_out * pieces[:, 5]).astype(jnp.bfloat16)
    grad_m_rows = lax.all_gather(grad_m_low, "tensor", axis=0, tiled=True).reshape(
        total_rows, width
    )
    fc2_bias_grad = jnp.sum(grad_m_rows, axis=0, dtype=jnp.float32)
    fc2_weight_grad = jnp.einsum(
        "rf,rd->fd", act_low, grad_m_rows, preferred_element_type=jnp.float32
    )
    act_grad = jnp.einsum("rd,fd->rf", grad_m_rows, w_fc2, preferred_element_type=jnp.float32)
    pre_grad = gelu_back(act_grad)[0].astype(jnp.bfloat16)
    fc1_bias_grad = jnp.sum(pre_grad, axis=0, dtype=jnp.float32)
    fc1_weight_grad = jnp.einsum("rd,rf->df", rows_m, pre_grad, preferred_element_type=jnp.float32)
    normed_m_grad = (
        lax.psum_scatter(
            jnp.einsum("rf,df->rd", pre_grad, w_fc1, preferred_element_type=jnp.float32).astype(
                jnp.bfloat16
            ),
            "tensor",
            scatter_dimension=0,
            tiled=True,
        )
        .astype(jnp.float32)
        .reshape(seq_local, latents, width)
    )
    resid_part, shift_m_grad, scale_m_grad = norm_m_back(normed_m_grad)
    resid_grad = grad_out + resid_part
    gate_a_grad = jnp.sum(resid_grad * attention_branch, axis=0)
    grad_a_low = (resid_grad * pieces[:, 2]).astype(jnp.bfloat16)
    grad_a_flat = grad_a_low.reshape(local_rows, width)
    proj_bias_part = jnp.sum(grad_a_flat, axis=0, dtype=jnp.float32)
    grad_a_rows = lax.all_gather(grad_a_low, "tensor", axis=0, tiled=True).reshape(
        total_rows, width
    )
    proj_weight_grad = jnp.einsum(
        "rc,rd->cd", attended_rows, grad_a_rows, preferred_element_type=jnp.float32
    )
    attended_grad = jnp.einsum(
        "rd,cd->rc", grad_a_rows, w_proj, preferred_element_type=jnp.float32
    ).astype(jnp.bfloat16)
    grad_packed = jnp.moveaxis(attended_grad.reshape(seq_len, latents, heads_here, head_size), 1, 0)
    qkv_grad_packed = lax.map(attend_backward, (packed, grad_packed, log_totals))
    qkv_grad_rows = jnp.moveaxis(qkv_grad_packed, 0, 1).reshape(total_rows, 3 * columns)
    bias_sums = jnp.sum(qkv_grad_rows.reshape(total_rows, 3, columns), axis=0, dtype=jnp.float32)
    qkv_bias_grad = jnp.stack([bias_sums[0], bias_sums[2]])
    qkv_weight_grad = jnp.einsum(
        "rd,rc->dc", rows_a, qkv_grad_rows, preferred_element_type=jnp.float32
    ).reshape(width, 3, columns)
    normed_a_grad = (
        lax.psum_scatter(
            jnp.einsum(
                "rc,dc->rd", qkv_grad_rows, qkv_flat, preferred_element_type=jnp.float32
            ).astype(jnp.bfloat16),
            "tensor",
            scatter_dimension=0,
            tiled=True,
        )
        .astype(jnp.float32)
        .reshape(seq_local, latents, width)
    )
    input_part, shift_a_grad, scale_a_grad = norm_a_back(normed_a_grad)
    tokens_grad = (resid_grad + input_part).astype(jnp.bfloat16)
    partial_mod = jnp.stack(
        [shift_a_grad, scale_a_grad, gate_a_grad, shift_m_grad, scale_m_grad, gate_m_grad], 1
    ).reshape(latents, 6 * width)
    mod_summed, proj_bias_grad = (
        lax.psum(partial_mod.astype(jnp.bfloat16), "tensor").astype(jnp.float32),
        lax.psum(proj_bias_part.astype(jnp.bfloat16), "tensor").astype(jnp.float32),
    )
    mod_grad_low = mod_summed.astype(jnp.bfloat16)
    silu_grad = jnp.einsum("le,de->ld", mod_grad_low, w_mod, preferred_element_type=jnp.float32)
    cond_grad = silu_back(silu_grad)[0]
    silu_every, mod_every = (
        lax.all_gather(silu_low, "dp", axis=0, tiled=True),
        lax.all_gather(mod_grad_low, "dp", axis=0, tiled=True),
    )
    owned_rows = mod_weight.shape[0]
    silu_owned = lax.dynamic_slice_in_dim(
        silu_every, lax.axis_index("dp") * owned_rows, owned_rows, 1
    )
    mod_weight_grad = jnp.einsum(
        "ld,le->de", silu_owned, mod_every, preferred_element_type=jnp.float32
    )
    mod_bias_grad = jnp.sum(mod_every, axis=0, dtype=jnp.float32)
    qkv_weight_grad, proj_weight_grad, fc1_weight_grad, fc2_weight_grad = (
        lax.psum_scatter(
            qkv_weight_grad.astype(jnp.bfloat16), "dp", scatter_dimension=0, tiled=True
        ).astype(jnp.float32),
        lax.psum_scatter(
            proj_weight_grad.astype(jnp.bfloat16), "dp", scatter_dimension=1, tiled=True
        ).astype(jnp.float32),
        lax.psum_scatter(
            fc1_weight_grad.astype(jnp.bfloat16), "dp", scatter_dimension=0, tiled=True
        ).astype(jnp.float32),
        lax.psum_scatter(
            fc2_weight_grad.astype(jnp.bfloat16), "dp", scatter_dimension=1, tiled=True
        ).astype(jnp.float32),
    )
    qkv_bias_grad, proj_bias_grad, fc1_bias_grad, fc2_bias_grad = lax.psum(
        (qkv_bias_grad, proj_bias_grad, fc1_bias_grad, fc2_bias_grad), "dp"
    )
    return (
        output,
        tokens_grad,
        cond_grad,
        mod_weight_grad,
        mod_bias_grad,
        qkv_weight_grad,
        qkv_bias_grad,
        proj_weight_grad,
        proj_bias_grad,
        fc1_weight_grad,
        fc1_bias_grad,
        fc2_weight_grad,
        fc2_bias_grad,
    )


def solution(mesh):
    return jax.shard_map(
        on_device,
        mesh=mesh,
        in_specs=(
            P("tensor", "dp", None),
            P("dp", None),
            P("dp", None),
            P(),
            P("dp", None, "tensor"),
            P(None, "tensor"),
            P("tensor", "dp"),
            P(),
            P("dp", "tensor"),
            P("tensor"),
            P("tensor", "dp"),
            P(),
            P("tensor", "dp", None),
        ),
        out_specs=(
            P("tensor", "dp", None),
            P("tensor", "dp", None),
            P("dp", None),
            P("dp", None),
            P(),
            P("dp", None, "tensor"),
            P(None, "tensor"),
            P("tensor", "dp"),
            P(),
            P("dp", "tensor"),
            P("tensor"),
            P("tensor", "dp"),
            P(),
        ),
        check_vma=False,
    )
```

profile of v0, /device:TPU:0, one launch (start us, length us, event | category | flops | bytes accessed | tf_op | source)
XLA Modules:
  0.0 1025.1 jit_solution(3620825164057800775)
XLA Ops:
  10.7 123.7 %all-gather.12.cloned.1.call-done = bf16[1152,6912]{1,0:T(8,128)(2,1)} async-done(((bf16[72,6912]{1,0:T(8,128)(2,1)}), bf16[1152,6912]{1,0:T(8,128)(2,1)}) %all-gather.12.cloned.1.call-update) | async-done | bytes 15925264 | tf_op jit(solution)/shard_map/all_gather | solution.py:106
  145.8 40.8 %all-gather.16.cloned.1.call-done = bf16[1152,3,576]{2,0,1:T(8,128)(2,1)} async-done(((bf16[72,3,576]{2,0,1:T(8,128)(2,1)}), bf16[1152,3,576]{2,0,1:T(8,128)(2,1)}) %all-gather.16.cloned.1.call-update) | async-done | bytes 3981328 | tf_op jit(solution)/shard_map/all_gather | solution.py:107
  193.1 30.2 %all-gather.14.cloned.1.call-done = bf16[1024,1,1152]{2,0,1:T(8,128)(2,1)} async-done(((bf16[512,1,1152]{2,0,1:T(8,128)(2,1)}), bf16[1024,1,1152]{2,0,1:T(8,128)(2,1)}) %all-gather.14.cloned.1.call-update) | async-done | bytes 2359312 | tf_op jit(solution)/shard_map/all_gather | solution.py:126
  241.7 13.6 %fusion.1 = f32[8,512]{1,0:T(8,128)S(1)} fusion(f32[8,512,1024]{2,1,0:T(8,128)} %get-tuple-element.73, f32[8,512]{1,0:T(8,128)S(1)} %get-tuple-element.72), kind=kLoop, calls=%fused_computation.11 | loop fusion | flops 12578816 | bytes 16809984 | tf_op jit(solution)/shard_map/while/body/eval_jaxpr/reduce_sum | solution.py:36
  278.3 34.3 %reduce-scatter.13.cloned.1.call-done = bf16[512,1152]{1,0:T(8,128)(2,1)} async-done(((bf16[1024,1152]{1,0:T(8,128)(2,1)}), bf16[512,1152]{1,0:T(8,128)(2,1)}) %reduce-scatter.13.cloned.1.call-update) | async-done | bytes 1179664 | tf_op jit(solution)/shard_map/reduce_scatter | solution.py:148
  321.7 49.5 %all-gather.22.cloned.1.call-done = bf16[1152,2304]{1,0:T(8,128)(2,1)} async-done(((bf16[72,2304]{1,0:T(8,128)(2,1)}), bf16[1152,2304]{1,0:T(8,128)(2,1)}) %all-gather.22.cloned.1.call-update) | async-done | bytes 5308432 | tf_op jit(solution)/shard_map/all_gather | solution.py:109
  371.2 36.9 %all-gather.20.cloned.1.call-done = bf16[1024,1,1152]{2,0,1:T(8,128)(2,1)} async-done(((bf16[512,1,1152]{2,0,1:T(8,128)(2,1)}), bf16[1024,1,1152]{2,0,1:T(8,128)(2,1)}) %all-gather.20.cloned.1.call-update) | async-done | bytes 2359312 | tf_op jit(solution)/shard_map/all_gather | solution.py:159
  419.7 47.1 %all-gather.24.cloned.1.call-done = bf16[2304,1152]{0,1:T(8,128)(2,1)} async-done(((bf16[2304,72]{0,1:T(8,128)(2,1)}), bf16[2304,1152]{0,1:T(8,128)(2,1)}) %all-gather.24.cloned.1.call-update) | async-done | bytes 5308432 | tf_op jit(solution)/shard_map/all_gather | solution.py:110
  466.9 36.9 %all-gather.26.cloned.1.call-done = bf16[1024,1,1152]{2,0,1:T(8,128)(2,1)} async-done(((bf16[512,1,1152]{2,0,1:T(8,128)(2,1)}), bf16[1024,1,1152]{2,0,1:T(8,128)(2,1)}) %all-gather.26.cloned.1.call-update) | async-done | bytes 2359312 | tf_op jit(solution)/shard_map/all_gather | solution.py:181
  503.7 15.4 %convert_reduce_fusion = (f32[2304]{0:T(1024)}, bf16[1024,2304]{1,0:T(8,128)(2,1)S(1)}) fusion(f32[1024,2304]{1,0:T(8,128)} %fusion.57, f32[2304]{0:T(1024)} %convert_element_type.198, bf16[2304,1152]{0,1:T(8,128)(2,1)} %all-gather.24.cloned.1.call-done, bf16[1024,1,1152]{2,0,1:T(8,128)(2,1)} %all-gather.26.cloned.1.call-done), kind=kOutput, calls=%fused_computation.27 | convolution fusion | flops 5490079744 | bytes 21841920 | tf_op jit(solution)/shard_map/rd,fd->rf/dot_general | solution.py:188
  531.8 34.4 %reduce-scatter.17.cloned.1.call-done = bf16[512,1152]{1,0:T(8,128)(2,1)} async-done(((bf16[1024,1152]{1,0:T(8,128)(2,1)}), bf16[512,1152]{1,0:T(8,128)(2,1)}) %reduce-scatter.17.cloned.1.call-update) | async-done | bytes 1179664 | tf_op jit(solution)/shard_map/reduce_scatter | solution.py:193
  596.0 13.1 %all-gather.28.cloned.1.call-done = bf16[1024,1,1152]{2,0,1:T(8,128)(2,1)} async-done(((bf16[512,1,1152]{2,0,1:T(8,128)(2,1)}), bf16[1024,1,1152]{2,0,1:T(8,128)(2,1)}) %all-gather.28.cloned.1.call-update) | async-done | bytes 2359312 | tf_op jit(solution)/shard_map/all_gather | solution.py:210
  613.5 15.2 %multiply_reduce_fusion.1 = (f32[8,512]{1,0:T(8,128)S(1)}, f32[8,512,1024]{2,1,0:T(8,128)}) fusion(f32[8,512,1024]{2,1,0:T(8,128)} %copy-done, f32[8,512]{1,0:T(8,128)S(1)} %log_add_fusion.1, bf16[512,8,72]{0,2,1:T(8,128)(2,1)S(1)} %bitcast.230, bf16[1024,3,8,72]{0,3,2,1:T(8,128)(2,1)} %bitcast.220), kind=kOutput, calls=%fused_computation.4 | convolution fusion | flops 620752896 | bytes 35356672 | tf_op jit(solution)/shard_map/while/body/eval_jaxpr/qhe,khe->hqk/dot_general | solution.py:66
  656.0 12.1 %multiply_reduce_fusion = (f32[8,512]{1,0:T(8,128)}, f32[8,512,1024]{2,1,0:T(8,128)}) fusion(f32[8,512,1024]{2,1,0:T(8,128)} %get-tuple-element.73, f32[8,512]{1,0:T(8,128)S(1)} %copy-done.29, bf16[512,8,72]{0,2,1:T(8,128)(2,1)S(1)} %bitcast.232, bf16[1024,3,8,72]{0,3,2,1:T(8,128)(2,1)S(1)} %bitcast.225), kind=kOutput, calls=%fused_computation.1 | convolution fusion | flops 620752896 | bytes 35356672 | tf_op jit(solution)/shard_map/while/body/eval_jaxpr/qhe,khe->hqk/dot_general | solution.py:66
  668.1 13.1 %multiply_convert_fusion = bf16[8,512,1024]{2,1,0:T(8,128)(2,1)S(1)} fusion(f32[8,512,1024]{2,1,0:T(8,128)} %get-tuple-element.79, f32[8,512,1024]{2,1,0:T(8,128)} %get-tuple-element.73, f32[8,512]{1,0:T(8,128)} %get-tuple-element.78, f32[8,512]{1,0:T(8,128)} %log_add_fusion), kind=kLoop, calls=%fused_computation | loop fusion | flops 20971520 | bytes 41975808 | tf_op jit(solution)/shard_map/while/body/eval_jaxpr/convert_element_type | solution.py:70
  719.4 13.8 %convolution_convert_fusion.4 = bf16[1024,1152]{1,0:T(8,128)(2,1)} fusion(bf16[2304,1152]{0,1:T(8,128)(2,1)} %all-gather.24.cloned.1.call-done, f32[1024,2304]{1,0:T(8,128)} %fusion.57, f32[2304]{0:T(1024)S(1)} %copy-done.59), kind=kOutput, calls=%fused_computation.45 | convolution fusion | flops 5460590592 | bytes 17114112 | tf_op jit(solution)/shard_map/dot_general | solution.py:169
  742.5 18.2 %copy.34 = bf16[1152,3,576]{2,1,0:T(4,128)(2,1)} copy(bf16[1152,3,576]{2,0,1:T(8,128)(2,1)S(1)} %convolution_convert_fusion.2) | data formatting | bytes 7962624
  760.7 12.3 %reshape.346 = bf16[1152,1728]{1,0:T(8,128)(2,1)} reshape(bf16[1152,3,576]{2,1,0:T(4,128)(2,1)} %copy.34) | data formatting | bytes 7962624
  774.3 21.5 %all-gather = bf16[16,1,1152]{2,1,0:T(2,128)(2,1)S(1)} all-gather(bf16[1,1,1152]{2,1,0:T(2,128)(2,1)S(1)} %convert_bitcast_fusion.2), channel_id=1, replica_groups=mesh['dp'=16,'tensor'=2] {'dp'}, dimensions={0}, use_global_device_ids=true | all-gather | bytes 39168 | tf_op jit(solution)/shard_map/all_gather | solution.py:252
  806.9 30.5 %reduce-scatter.27.cloned.1.call-done = bf16[576,72]{0,1:T(8,128)(2,1)} async-done(((bf16[576,1152]{0,1:T(8,128)(2,1)}), bf16[576,72]{0,1:T(8,128)(2,1)}) %reduce-scatter.27.cloned.1.call-update) | async-done | bytes 82960
  839.0 34.2 %reduce-scatter.19.cloned.1.call-done = bf16[512,1152]{1,0:T(8,128)(2,1)} async-done(((bf16[1024,1152]{1,0:T(8,128)(2,1)}), bf16[512,1152]{1,0:T(8,128)(2,1)}) %reduce-scatter.19.cloned.1.call-update) | async-done | bytes 1179664 | tf_op jit(solution)/shard_map/reduce_scatter | solution.py:228
  881.7 28.4 %reduce-scatter.15.cloned.1.call-done = bf16[512,1152]{1,0:T(8,128)(2,1)} async-done(((bf16[1024,1152]{1,0:T(8,128)(2,1)}), bf16[512,1152]{1,0:T(8,128)(2,1)}) %reduce-scatter.15.cloned.1.call-update) | async-done | bytes 1179664 | tf_op jit(solution)/shard_map/reduce_scatter | solution.py:168
  923.8 60.7 %all-reduce.1 = (f32[2,576]{1,0:T(2,128)}, f32[1152]{0:T(1024)}, f32[2304]{0:T(1024)}, f32[1152]{0:T(1024)}) all-reduce(f32[2,576]{1,0:T(2,128)} %pad_maximum_fusion.5, bf16[1152]{0:T(1024)(128)(2,1)S(1)} %get-tuple-element.57, f32[2304]{0:T(1024)} %get-tuple-element.80, ...), channel_id=1, replica_groups=mesh['dp'=16,'tensor'=2] {'dp'}, use_global_device_ids=true, to_apply=%region_28.29 | all-reduce | flops 5760 | bytes 43776 | tf_op jit(solution)/shard_map/psum | solution.py:277
  984.5 18.4 %all-gather.1 = bf16[16,1,6912]{2,1,0:T(2,128)(2,1)S(1)} all-gather(bf16[1,1,6912]{2,1,0:T(2,128)(2,1)S(1)} %bitcast.239), channel_id=1, replica_groups=mesh['dp'=16,'tensor'=2] {'dp'}, dimensions={0}, use_global_device_ids=true | all-gather | bytes 235008 | tf_op jit(solution)/shard_map/all_gather | solution.py:253
  (284 shorter events, 255.9 us)
Async XLA Ops:
  7.2 127.3 %copy-start.46 = (bf16[1,1152]{1,0:T(2,128)(2,1)S(1)}, bf16[1,1152]{1,0:T(2,128)(2,1)}, u32[]{:S(2)}) copy-start(bf16[1,1152]{1,0:T(2,128)(2,1)} %param.14) | copy-start | bytes 6916
  7.2 127.3 %all-gather.12.cloned.1.call-start = ((), (), s32[]{:S(2)}) async-start(), calls=%async_computation.8 | async-start | bytes 16920576 | tf_op jit(solution)/shard_map/all_gather | solution.py:106
  7.9 178.7 %all-gather.16.cloned.1.call-start = ((), (), s32[]{:S(2)}) async-start(), calls=%async_computation.10 | async-start | bytes 4700160 | tf_op jit(solution)/shard_map/all_gather | solution.py:107
  8.7 214.7 %all-gather.14.cloned.1.call-start = ((), (), s32[]{:S(2)}) async-start(), calls=%async_computation.9 | async-start | bytes 3538944 | tf_op jit(solution)/shard_map/all_gather | solution.py:126
  10.2 132.7 %copy-start.38 = (f32[512]{0:T(512)}, f32[512]{0:T(512)S(1)}, u32[]{:S(2)}) copy-start(f32[512]{0:T(512)S(1)} %broadcast_multiply_fusion.1) | copy-start | bytes 6148
  10.7 123.8 %copy-start.53 = (f32[512]{0:T(512)}, f32[512]{0:T(512)S(1)}, u32[]{:S(2)}) copy-start(f32[512]{0:T(512)S(1)} %fusion.42) | copy-start | bytes 6148
  10.7 132.2 %copy-start.43 = (f32[512]{0:T(512)}, f32[512]{0:T(512)S(1)}, u32[]{:S(2)}) copy-start(f32[512]{0:T(512)S(1)} %fusion.96) | copy-start | bytes 6148
  10.7 131.5 %copy-start.58 = (bf16[6912]{0:T(1024)(128)(2,1)S(1)}, bf16[6912]{0:T(1024)(128)(2,1)}, u32[]{:S(2)}) copy-start(bf16[6912]{0:T(1024)(128)(2,1)} %param.16) | copy-start | bytes 41476
  142.9 427.8 %copy-start.25 = (f32[1152]{0:T(1024)}, f32[1152]{0:T(1024)S(1)}, u32[]{:S(2)}) copy-start(f32[1152]{0:T(1024)S(1)} %get-tuple-element.51) | copy-start | bytes 13828
  144.5 127.9 %all-gather.18.cloned.1.call-start = ((), (), s32[]{:S(2)}) async-start(), calls=%async_computation.11 | async-start | bytes 1566720 | tf_op jit(solution)/shard_map/all_gather | solution.py:108
  145.0 167.5 %reduce-scatter.13.cloned.1.call-start = ((), (), s32[]{:S(2)}) async-start(), calls=%async_computation.12 | async-start | bytes 3538944 | tf_op jit(solution)/shard_map/reduce_scatter | solution.py:148
  277.6 93.6 %all-gather.22.cloned.1.call-start = ((), (), s32[]{:S(2)}) async-start(), calls=%async_computation.14 | async-start | bytes 5640192 | tf_op jit(solution)/shard_map/all_gather | solution.py:109
  278.2 129.9 %all-gather.20.cloned.1.call-start = ((), (), s32[]{:S(2)}) async-start(), calls=%async_computation.13 | async-start | bytes 3538944 | tf_op jit(solution)/shard_map/all_gather | solution.py:159
  278.3 291.3 %copy-start.27 = (f32[1152]{0:T(1024)}, f32[1152]{0:T(1024)S(1)}, u32[]{:S(2)}) copy-start(f32[1152]{0:T(1024)S(1)} %convert_element_type.196) | copy-start | bytes 13828
  317.6 149.3 %all-gather.24.cloned.1.call-start = ((), (), s32[]{:S(2)}) async-start(), calls=%async_computation.15 | async-start | bytes 5640192 | tf_op jit(solution)/shard_map/all_gather | solution.py:110
  318.4 185.4 %all-gather.26.cloned.1.call-start = ((), (), s32[]{:S(2)}) async-start(), calls=%async_computation.17 | async-start | bytes 3538944 | tf_op jit(solution)/shard_map/all_gather | solution.py:181
  320.4 245.9 %reduce-scatter.17.cloned.1.call-start = ((), (), s32[]{:S(2)}) async-start(), calls=%async_computation.18 | async-start | bytes 3538944 | tf_op jit(solution)/shard_map/reduce_scatter | solution.py:193
  531.4 77.8 %all-gather.28.cloned.1.call-start = ((), (), s32[]{:S(2)}) async-start(), calls=%async_computation.19 | async-start | bytes 3538944 | tf_op jit(solution)/shard_map/all_gather | solution.py:210
  572.9 230.2 %reduce-scatter.23.cloned.1.call-start = ((), (), s32[]{:S(2)}) async-start(), calls=%async_computation.22 | async-start | bytes 5640192 | tf_op jit(solution)/shard_map/reduce_scatter | solution.py:273
  584.6 220.4 %reduce-scatter.21.cloned.1.call-start = ((), (), s32[]{:S(2)}) async-start(), calls=%async_computation.21 | async-start | bytes 5640192 | tf_op jit(solution)/shard_map/reduce_scatter | solution.py:270
  596.0 241.4 %reduce-scatter.27.cloned.1.call-start = ((), (), s32[]{:S(2)}) async-start(), calls=%async_computation.24 | async-start | bytes 1566720
  700.8 172.4 %reduce-scatter.19.cloned.1.call-start = ((), (), s32[]{:S(2)}) async-start(), calls=%async_computation.20 | async-start | bytes 3538944 | tf_op jit(solution)/shard_map/reduce_scatter | solution.py:228
  718.7 191.5 %reduce-scatter.15.cloned.1.call-start = ((), (), s32[]{:S(2)}) async-start(), calls=%async_computation.16 | async-start | bytes 3538944 | tf_op jit(solution)/shard_map/reduce_scatter | solution.py:168
  733.2 283.2 %reduce-scatter.25.cloned.1.call-start = ((), (), s32[]{:S(2)}) async-start(), calls=%async_computation.23 | async-start | bytes 4386816
  (73 other events, 861.3 us)
Sparse Core Ops, SparseCore 0:
  10.2 124.2 all-gather.11
  136.7 49.9 all-gather.15
  188.7 34.5 all-gather.13
  225.3 39.3 all-gather.17
  277.7 34.7 reduce-scatter.12
  314.8 56.3 all-gather.21
  373.4 34.6 all-gather.19
  410.5 56.3 all-gather.23
  469.1 34.6 all-gather.25
  531.5 34.6 reduce-scatter.16
  573.0 36.0 all-gather.27
  613.0 79.7 reduce-scatter.22
  696.9 78.7 reduce-scatter.20
  779.8 57.5 reduce-scatter.26
  839.5 33.6 reduce-scatter.18
  875.4 34.6 reduce-scatter.14
  913.9 72.8 reduce-scatter.24
where the time goes:
time: 1030 us
  waiting for transfers between devices  543 us (53%)
  matrix products  207 us (20%)
  blocking collectives  108 us (10%)
  other arithmetic  87 us (8%)
  local copies, waits for them, and re-layouts  62.4 us (6%)
  between operations  14.9 us (1%)
    all_gather x1, waiting for transfers between devices, on_device(): lax.all_gather(mod_weight, 'dp', axis=0, tiled=True)  124 us
    psum x1, blocking collectives, on_device(): lax.psum((qkv_bias_grad, proj_bias_grad, fc1_bias_grad, fc2_bias_grad), '...  60.7 us
    unnamed x164, local copies, waits for them, and re-layouts  51 us
    all_gather x1, waiting for transfers between devices, on_device(): lax.all_gather(first_hidden_weight, 'dp', axis=0, tiled=True)  49.5 us
    all_gather x1, waiting for transfers between devices, on_device(): lax.all_gather(second_hidden_weight, 'dp', axis=1, tiled=True)  47.1 us
    all_gather x1, waiting for transfers between devices, on_device(): lax.all_gather(query_key_value_weight, 'dp', axis=0, tiled=True)  40.8 us
    all_gather x1, waiting for transfers between devices, on_device(): lax.all_gather(grad_m_low, 'tensor', axis=0, tiled=True)  36.9 us
    all_gather x1, waiting for transfers between devices, on_device(): lax.all_gather(feedforward_normalized.astype(jnp.bfloat16), 'tensor', axi...  36.9 us
  transfers between devices with their start and end apart: 17, of which 13 were waited for; matrix products, arithmetic and copies ran while one was open for 29% of the time, Pallas kernels for 0%

commit v1 on v0

--- a/solution.py
+++ b/solution.py
@@ -2,8 +2,30 @@
 import jax.numpy as jnp
 from jax import lax
 from jax.sharding import PartitionSpec as P
+from jax.lax import axis_index, axis_size, ppermute
 
 HEADS = 16
+
+
+def lead_the_task(target, mesh_ax):
+    z2 = axis_size(mesh_ax)
+    step_out = axis_index(mesh_ax)
+    r2, y2, new = (z2, step_out, target.shape[0])
+    in_order = [src_i * r2 if at == 0 else src_i for at, src_i in enumerate(target.shape)]
+    passed = jnp.zeros(in_order, target.dtype)
+    local_next = vec_out = target
+    t1 = lax.dynamic_update_slice_in_dim(passed, target, y2 * new, axis=0)
+    for kk in range(1, r2 // 2 + 1):
+        f_now = range(r2)
+        odd = map(lambda at: (at, (at + 1) % r2), f_now)
+        local_next = ppermute(local_next, mesh_ax, perm=list(odd))
+        t1 = lax.dynamic_update_slice_in_dim(t1, local_next, (y2 - kk) % r2 * new, axis=0)
+        if 2 * kk < r2:
+            vec_out = ppermute(
+                vec_out, mesh_ax, perm=list(map(lambda at: (at, (at - 1) % r2), range(r2)))
+            )
+            t1 = lax.dynamic_update_slice_in_dim(t1, vec_out, (y2 + kk) % r2 * new, axis=0)
+    return t1
 
 
 def modulate(hidden, shifts, scales):
@@ -106,7 +128,7 @@
         lax.all_gather(mod_weight, "dp", axis=0, tiled=True),
         lax.all_gather(query_key_value_weight, "dp", axis=0, tiled=True),
         lax.all_gather(attention_out_weight, "dp", axis=1, tiled=True),
-        lax.all_gather(first_hidden_weight, "dp", axis=0, tiled=True),
+        lead_the_task(first_hidden_weight, "dp"),
         lax.all_gather(second_hidden_weight, "dp", axis=1, tiled=True),
     )
     seq_local, latents, width = tokens.shape

time: 1030 us -> 988 us (0.959)
  waiting for transfers between devices: 543 us -> 441 us
  starting transfers between devices: 1.62 us -> 33.2 us
  local copies, waits for them, and re-layouts: 62.4 us -> 77.5 us
    all_gather x1 -> x0, waiting for transfers between devices: 49.5 us -> none  [on_device(): lax.all_gather(first_hidden_weight, 'dp', axis=0, tiled=True)]
    all_gather x1, waiting for transfers between devices: 47.1 us -> 0.01 us  [on_device(): lax.all_gather(second_hidden_weight, 'dp', axis=1, tiled=True)]
    ppermute x0 -> x15, waiting for transfers between devices: none -> 38.4 us  [the longest x8 19.6 us: lead_the_task(): local_next = ppermute(local_next, mesh_ax, perm=list(odd))]
    all_gather x1, waiting for transfers between devices: 36.9 us -> 0.01 us  [on_device(): lax.all_gather(feedforward_normalized.astype(jnp.bfloat16), 'tensor', axi...]
    ppermute x0 -> x15, starting transfers between devices: none -> 31.7 us  [the longest x7 31.6 us: lead_the_task(): ppermute(vec_out, mesh_ax, perm=list(map(lambda at: (at, (at - 1) % r2),...]
    dynamic_update_slice x0 -> x16, local copies, waits for them, and re-layouts: none -> 19 us  [the longest x8 8.98 us: lead_the_task(): lax.dynamic_update_slice_in_dim(t1, local_next, (y2 - kk) % r2 * new, axi...]
    unnamed x164 -> x156, local copies, waits for them, and re-layouts: 51 us -> 43.6 us
    unnamed x19 -> x18, waiting for transfers between devices: 33.8 us -> 30.2 us
  transfers between devices with their start and end apart: 17 -> 31, of which waited for: 13 -> 19; matrix products, arithmetic and copies ran while one was open for 29% -> 33% of each run, Pallas kernels for 0% -> 0%
where the time goes in v1:
time: 988 us; the launch traced here: 982 us
  waiting for transfers between devices  441 us (45%)
  matrix products  214 us (22%)
  blocking collectives  108 us (11%)
  other arithmetic  93.4 us (9%)
  local copies, waits for them, and re-layouts  77.5 us (8%)
  starting transfers between devices  33.2 us (3%)
  between operations  14.9 us (2%)
    all_gather x1, waiting for transfers between devices, on_device(): lax.all_gather(mod_weight, 'dp', axis=0, tiled=True)  122 us
    psum x1, blocking collectives, on_device(): lax.psum((qkv_bias_grad, proj_bias_grad, fc1_bias_grad, fc2_bias_grad), '...  60.8 us
    unnamed x156, local copies, waits for them, and re-layouts  43.6 us
    all_gather x1, waiting for transfers between devices, on_device(): lax.all_gather(query_key_value_weight, 'dp', axis=0, tiled=True)  40.8 us
    reduce_scatter x1, waiting for transfers between devices, on_device(): lax.psum_scatter(jnp.dot(attended_rows, w_proj, preferred_element_type=jn...  34.8 us
    all_gather x1, waiting for transfers between devices, on_device(): lax.all_gather(grad_m_low, 'tensor', axis=0, tiled=True)  34.6 us
    reduce_scatter x1, waiting for transfers between devices, on_device(): lax.psum_scatter(jnp.einsum('rf,df->rd', pre_grad, w_fc1, preferred_eleme...  34.4 us
    reduce_scatter x1, waiting for transfers between devices, on_device(): lax.psum_scatter(jnp.einsum('rc,dc->rd', qkv_grad_rows, qkv_flat, preferr...  34.2 us
  transfers between devices with their start and end apart: 31, of which 19 were waited for; matrix products, arithmetic and copies ran while one was open for 33% of the time, Pallas kernels for 0%

profile of v1, /device:TPU:0, one launch (start us, length us, event | category | flops | bytes accessed | tf_op | source)
XLA Modules:
  0.0 982.4 jit_solution(10997163675689833448)
XLA Ops:
  12.0 122.4 %all-gather.11.cloned.1.call-done = bf16[1152,6912]{1,0:T(8,128)(2,1)} async-done(((bf16[72,6912]{1,0:T(8,128)(2,1)}), bf16[1152,6912]{1,0:T(8,128)(2,1)}) %all-gather.11.cloned.1.call-update) | async-done | bytes 15925264 | tf_op jit(solution)/shard_map/all_gather | solution.py:128
  145.8 40.8 %all-gather.15.cloned.1.call-done = bf16[1152,3,576]{2,0,1:T(8,128)(2,1)} async-done(((bf16[72,3,576]{2,0,1:T(8,128)(2,1)}), bf16[1152,3,576]{2,0,1:T(8,128)(2,1)}) %all-gather.15.cloned.1.call-update) | async-done | bytes 3981328 | tf_op jit(solution)/shard_map/all_gather | solution.py:129
  193.2 30.1 %all-gather.13.cloned.1.call-done = bf16[1024,1,1152]{2,0,1:T(8,128)(2,1)} async-done(((bf16[512,1,1152]{2,0,1:T(8,128)(2,1)}), bf16[1024,1,1152]{2,0,1:T(8,128)(2,1)}) %all-gather.13.cloned.1.call-update) | async-done | bytes 2359312 | tf_op jit(solution)/shard_map/all_gather | solution.py:148
  241.7 13.6 %fusion.1 = f32[8,512]{1,0:T(8,128)S(1)} fusion(f32[8,512,1024]{2,1,0:T(8,128)} %get-tuple-element.73, f32[8,512]{1,0:T(8,128)S(1)} %get-tuple-element.72), kind=kLoop, calls=%fused_computation.11 | loop fusion | flops 12578816 | bytes 16809984 | tf_op jit(solution)/shard_map/while/body/eval_jaxpr/reduce_sum | solution.py:58
  277.7 34.8 %reduce-scatter.13.cloned.1.call-done = bf16[512,1152]{1,0:T(8,128)(2,1)} async-done(((bf16[1024,1152]{1,0:T(8,128)(2,1)}), bf16[512,1152]{1,0:T(8,128)(2,1)}) %reduce-scatter.13.cloned.1.call-update) | async-done | bytes 1179664 | tf_op jit(solution)/shard_map/reduce_scatter | solution.py:170
  412.9 11.8 %fusion.57 = f32[1024,2304]{1,0:T(8,128)} fusion(bf16[1152,2304]{1,0:T(8,128)(2,1)} %constant_dynamic-update-slice_fusion, bf16[1024,1,1152]{2,0,1:T(8,128)(2,1)} %all-gather.19.cloned.1.call-done), kind=kOutput, calls=%fused_computation.98 | convolution fusion | flops 5435817984 | bytes 17104896 | tf_op jit(solution)/shard_map/dot_general | solution.py:185
  424.8 34.6 %all-gather.23.cloned.1.call-done = bf16[1024,1,1152]{2,0,1:T(8,128)(2,1)} async-done(((bf16[512,1,1152]{2,0,1:T(8,128)(2,1)}), bf16[1024,1,1152]{2,0,1:T(8,128)(2,1)}) %all-gather.23.cloned.1.call-update) | async-done | bytes 2359312 | tf_op jit(solution)/shard_map/all_gather | solution.py:203
  459.3 15.4 %convert_reduce_fusion = (f32[2304]{0:T(1024)}, bf16[1024,2304]{1,0:T(8,128)(2,1)S(1)}) fusion(f32[1024,2304]{1,0:T(8,128)} %fusion.57, f32[2304]{0:T(1024)} %convert_element_type.198, bf16[2304,1152]{0,1:T(8,128)(2,1)} %all-gather.21.cloned.1.call-done, bf16[1024,1,1152]{2,0,1:T(8,128)(2,1)} %all-gather.23.cloned.1.call-done), kind=kOutput, calls=%fused_computation.27 | convolution fusion | flops 5490079744 | bytes 21841920 | tf_op jit(solution)/shard_map/rd,fd->rf/dot_general | solution.py:210
  487.4 34.4 %reduce-scatter.17.cloned.1.call-done = bf16[512,1152]{1,0:T(8,128)(2,1)} async-done(((bf16[1024,1152]{1,0:T(8,128)(2,1)}), bf16[512,1152]{1,0:T(8,128)(2,1)}) %reduce-scatter.17.cloned.1.call-update) | async-done | bytes 1179664 | tf_op jit(solution)/shard_map/reduce_scatter | solution.py:215
  530.0 10.9 %convolution_convert_fusion = bf16[2304,1152]{0,1:T(8,128)(2,1)} fusion(bf16[1024,1,1152]{2,0,1:T(8,128)(2,1)S(1)} %copy-done.22, f32[1024,2304]{1,0:T(8,128)} %fusion.57, f32[2304]{0:T(1024)} %convert_element_type.198), kind=kOutput, calls=%fused_computation.16 | convolution fusion | flops 5462065152 | bytes 17114112 | tf_op jit(solution)/shard_map/rf,rd->fd/dot_general | solution.py:207
  552.4 13.8 %all-gather.25.cloned.1.call-done = bf16[1024,1,1152]{2,0,1:T(8,128)(2,1)} async-done(((bf16[512,1,1152]{2,0,1:T(8,128)(2,1)}), bf16[1024,1,1152]{2,0,1:T(8,128)(2,1)}) %all-gather.25.cloned.1.call-update) | async-done | bytes 2359312 | tf_op jit(solution)/shard_map/all_gather | solution.py:232
  570.5 15.2 %multiply_reduce_fusion.1 = (f32[8,512]{1,0:T(8,128)S(1)}, f32[8,512,1024]{2,1,0:T(8,128)}) fusion(f32[8,512,1024]{2,1,0:T(8,128)} %copy-done, f32[8,512]{1,0:T(8,128)S(1)} %log_add_fusion.1, bf16[512,8,72]{0,2,1:T(8,128)(2,1)S(1)} %bitcast.230, bf16[1024,3,8,72]{0,3,2,1:T(8,128)(2,1)} %bitcast.220), kind=kOutput, calls=%fused_computation.4 | convolution fusion | flops 620752896 | bytes 35356672 | tf_op jit(solution)/shard_map/while/body/eval_jaxpr/qhe,khe->hqk/dot_general | solution.py:88
  588.7 11.0 %multiply_convert_fusion.1 = bf16[8,512,1024]{2,1,0:T(8,128)(2,1)} fusion(f32[8,512,1024]{2,1,0:T(8,128)} %get-tuple-element.77, f32[8,512,1024]{2,1,0:T(8,128)S(1)} %bitcast.213, f32[8,512]{1,0:T(8,128)S(1)} %get-tuple-element.76, f32[8,512]{1,0:T(8,128)S(1)} %log_add_fusion.1), kind=kLoop, calls=%fused_computation.3 | loop fusion | flops 20971520 | bytes 41975808 | tf_op jit(solution)/shard_map/while/body/eval_jaxpr/convert_element_type | solution.py:92
  613.0 11.5 %multiply_reduce_fusion = (f32[8,512]{1,0:T(8,128)S(1)}, f32[8,512,1024]{2,1,0:T(8,128)}) fusion(f32[8,512,1024]{2,1,0:T(8,128)} %get-tuple-element.73, f32[8,512]{1,0:T(8,128)S(1)} %copy-done.27, bf16[512,8,72]{0,2,1:T(8,128)(2,1)S(1)} %bitcast.232, bf16[1024,3,8,72]{0,3,2,1:T(8,128)(2,1)S(1)} %bitcast.223), kind=kOutput, calls=%fused_computation.1 | convolution fusion | flops 620752896 | bytes 35356672 | tf_op jit(solution)/shard_map/while/body/eval_jaxpr/qhe,khe->hqk/dot_general | solution.py:88
  624.5 16.3 %multiply_convert_fusion = bf16[8,512,1024]{2,1,0:T(8,128)(2,1)} fusion(f32[8,512,1024]{2,1,0:T(8,128)} %get-tuple-element.79, f32[8,512,1024]{2,1,0:T(8,128)} %get-tuple-element.73, f32[8,512]{1,0:T(8,128)S(1)} %get-tuple-element.78, f32[8,512]{1,0:T(8,128)S(1)} %copy-done.27), kind=kLoop, calls=%fused_computation | loop fusion | flops 20971520 | bytes 41975808 | tf_op jit(solution)/shard_map/while/body/eval_jaxpr/convert_element_type | solution.py:92
  680.4 14.5 %convolution_convert_fusion.4 = bf16[1024,1152]{1,0:T(8,128)(2,1)} fusion(bf16[2304,1152]{0,1:T(8,128)(2,1)} %all-gather.21.cloned.1.call-done, f32[1024,2304]{1,0:T(8,128)} %fusion.57, f32[2304]{0:T(1024)S(1)} %copy-done.55), kind=kOutput, calls=%fused_computation.45 | convolution fusion | flops 5460590592 | bytes 17114112 | tf_op jit(solution)/shard_map/dot_general | solution.py:191
  702.8 18.2 %copy.34 = bf16[1152,3,576]{2,1,0:T(4,128)(2,1)} copy(bf16[1152,3,576]{2,0,1:T(8,128)(2,1)S(1)} %convolution_convert_fusion.2) | data formatting | bytes 7962624
  721.1 12.3 %reshape.346 = bf16[1152,1728]{1,0:T(8,128)(2,1)} reshape(bf16[1152,3,576]{2,1,0:T(4,128)(2,1)} %copy.34) | data formatting | bytes 7962624
  734.7 21.5 %all-gather = bf16[16,1,1152]{2,1,0:T(2,128)(2,1)S(1)} all-gather(bf16[1,1,1152]{2,1,0:T(2,128)(2,1)S(1)} %convert_bitcast_fusion.2), channel_id=1, replica_groups=mesh['dp'=16,'tensor'=2] {'dp'}, dimensions={0}, use_global_device_ids=true | all-gather | bytes 39168 | tf_op jit(solution)/shard_map/all_gather | solution.py:274
  767.3 27.4 %reduce-scatter.27.cloned.1.call-done = bf16[576,72]{0,1:T(8,128)(2,1)} async-done(((bf16[576,1152]{0,1:T(8,128)(2,1)}), bf16[576,72]{0,1:T(8,128)(2,1)}) %reduce-scatter.27.cloned.1.call-update) | async-done | bytes 82960
  796.2 34.2 %reduce-scatter.19.cloned.1.call-done = bf16[512,1152]{1,0:T(8,128)(2,1)} async-done(((bf16[1024,1152]{1,0:T(8,128)(2,1)}), bf16[512,1152]{1,0:T(8,128)(2,1)}) %reduce-scatter.19.cloned.1.call-update) | async-done | bytes 1179664 | tf_op jit(solution)/shard_map/reduce_scatter | solution.py:250
  840.2 27.2 %reduce-scatter.15.cloned.1.call-done = bf16[512,1152]{1,0:T(8,128)(2,1)} async-done(((bf16[1024,1152]{1,0:T(8,128)(2,1)}), bf16[512,1152]{1,0:T(8,128)(2,1)}) %reduce-scatter.15.cloned.1.call-update) | async-done | bytes 1179664 | tf_op jit(solution)/shard_map/reduce_scatter | solution.py:190
  881.1 60.8 %all-reduce.1 = (f32[2,576]{1,0:T(2,128)}, f32[1152]{0:T(1024)}, f32[2304]{0:T(1024)}, f32[1152]{0:T(1024)}) all-reduce(f32[2,576]{1,0:T(2,128)} %pad_maximum_fusion.5, bf16[1152]{0:T(1024)(128)(2,1)S(1)} %get-tuple-element.57, f32[2304]{0:T(1024)} %get-tuple-element.80, ...), channel_id=1, replica_groups=mesh['dp'=16,'tensor'=2] {'dp'}, use_global_device_ids=true, to_apply=%region_28.29 | all-reduce | flops 5760 | bytes 43776 | tf_op jit(solution)/shard_map/psum | solution.py:299
  941.9 18.4 %all-gather.1 = bf16[16,1,6912]{2,1,0:T(2,128)(2,1)S(1)} all-gather(bf16[1,1,6912]{2,1,0:T(2,128)(2,1)S(1)} %bitcast.239), channel_id=1, replica_groups=mesh['dp'=16,'tensor'=2] {'dp'}, dimensions={0}, use_global_device_ids=true | all-gather | bytes 235008 | tf_op jit(solution)/shard_map/all_gather | solution.py:275
  (320 shorter events, 316.3 us)
Async XLA Ops:
  7.2 127.3 %all-gather.11.cloned.1.call-start = ((), (), s32[]{:S(2)}) async-start(), calls=%async_computation.8 | async-start | bytes 16920576 | tf_op jit(solution)/shard_map/all_gather | solution.py:128
  7.9 178.7 %all-gather.15.cloned.1.call-start = ((), (), s32[]{:S(2)}) async-start(), calls=%async_computation.10 | async-start | bytes 4700160 | tf_op jit(solution)/shard_map/all_gather | solution.py:129
  8.7 214.7 %all-gather.13.cloned.1.call-start = ((), (), s32[]{:S(2)}) async-start(), calls=%async_computation.9 | async-start | bytes 3538944 | tf_op jit(solution)/shard_map/all_gather | solution.py:148
  144.4 127.9 %all-gather.17.cloned.1.call-start = ((), (), s32[]{:S(2)}) async-start(), calls=%async_computation.11 | async-start | bytes 1566720 | tf_op jit(solution)/shard_map/all_gather | solution.py:130
  145.0 167.5 %reduce-scatter.13.cloned.1.call-start = ((), (), s32[]{:S(2)}) async-start(), calls=%async_computation.12 | async-start | bytes 3538944 | tf_op jit(solution)/shard_map/reduce_scatter | solution.py:170
  277.6 135.3 %all-gather.19.cloned.1.call-start = ((), (), s32[]{:S(2)}) async-start(), calls=%async_computation.13 | async-start | bytes 3538944 | tf_op jit(solution)/shard_map/all_gather | solution.py:181
  318.3 106.4 %all-gather.21.cloned.1.call-start = ((), (), s32[]{:S(2)}) async-start(), calls=%async_computation.14 | async-start | bytes 5640192 | tf_op jit(solution)/shard_map/all_gather | solution.py:132
  319.1 140.2 %all-gather.23.cloned.1.call-start = ((), (), s32[]{:S(2)}) async-start(), calls=%async_computation.16 | async-start | bytes 3538944 | tf_op jit(solution)/shard_map/all_gather | solution.py:203
  322.9 9.7 collective-permute-start
  328.1 9.4 collective-permute-start.3
  332.5 9.6 collective-permute-start.2
  365.4 14.3 %collective-permute-start.11 = (bf16[72,2304]{1,0:T(8,128)(2,1)S(1)}, bf16[72,2304]{1,0:T(8,128)(2,1)}, u32[]{:S(2)}, u32[]{:S(2)}) collective-permute-start(bf16[72,2304]{1,0:T(8,128)(2,1)S(1)} %collective-permute-done.9), channel_id=1, source_target_pairs={{0,30},{2,0},{4,2},{6,4},{8,6},{10,8},{12,10},{14,12},{16,14},{18,... | collective-permute-start | bytes 995336 | tf_op jit(solution)/shard_map/ppermute | solution.py:24
  370.2 15.4 %collective-permute-start.10 = (bf16[72,2304]{1,0:T(8,128)(2,1)S(1)}, bf16[72,2304]{1,0:T(8,128)(2,1)}, u32[]{:S(2)}, u32[]{:S(2)}) collective-permute-start(bf16[72,2304]{1,0:T(8,128)(2,1)S(1)} %collective-permute-done.8), channel_id=1, source_target_pairs={{0,2},{2,4},{4,6},{6,8},{8,10},{10,12},{12,14},{14,16},{16,18},{18... | collective-permute-start | bytes 995336 | tf_op jit(solution)/shard_map/ppermute | solution.py:21
  379.8 21.7 %collective-permute-start.13 = (bf16[72,2304]{1,0:T(8,128)(2,1)}, bf16[72,2304]{1,0:T(8,128)(2,1)}, u32[]{:S(2)}, u32[]{:S(2)}) collective-permute-start(bf16[72,2304]{1,0:T(8,128)(2,1)} %collective-permute-done.11), channel_id=1, source_target_pairs={{0,30},{2,0},{4,2},{6,4},{8,6},{10,8},{12,10},{14,12},{16,14},{18,... | collective-permute-start | bytes 995336 | tf_op jit(solution)/shard_map/ppermute | solution.py:24
  385.6 14.1 %collective-permute-start.12 = (bf16[72,2304]{1,0:T(8,128)(2,1)}, bf16[72,2304]{1,0:T(8,128)(2,1)}, u32[]{:S(2)}, u32[]{:S(2)}) collective-permute-start(bf16[72,2304]{1,0:T(8,128)(2,1)} %collective-permute-done.10), channel_id=1, source_target_pairs={{0,2},{2,4},{4,6},{6,8},{8,10},{10,12},{12,14},{14,16},{16,18},{18... | collective-permute-start | bytes 995336 | tf_op jit(solution)/shard_map/ppermute | solution.py:21
  388.6 133.3 %reduce-scatter.17.cloned.1.call-start = ((), (), s32[]{:S(2)}) async-start(), calls=%async_computation.17 | async-start | bytes 3538944 | tf_op jit(solution)/shard_map/reduce_scatter | solution.py:215
  399.7 12.5 %collective-permute-start.14 = (bf16[72,2304]{1,0:T(8,128)(2,1)}, bf16[72,2304]{1,0:T(8,128)(2,1)S(1)}, u32[]{:S(2)}, u32[]{:S(2)}) collective-permute-start(bf16[72,2304]{1,0:T(8,128)(2,1)} %collective-permute-done.12), channel_id=1, source_target_pairs={{0,2},{2,4},{4,6},{6,8},{8,10},{10,12},{12,14},{14,16},{16,18},{18... | collective-permute-start | bytes 995336 | tf_op jit(solution)/shard_map/ppermute | solution.py:21
  487.0 79.2 %all-gather.25.cloned.1.call-start = ((), (), s32[]{:S(2)}) async-start(), calls=%async_computation.18 | async-start | bytes 3538944 | tf_op jit(solution)/shard_map/all_gather | solution.py:232
  529.9 233.5 %reduce-scatter.23.cloned.1.call-start = ((), (), s32[]{:S(2)}) async-start(), calls=%async_computation.21 | async-start | bytes 5640192 | tf_op jit(solution)/shard_map/reduce_scatter | solution.py:295
  540.9 224.4 %reduce-scatter.21.cloned.1.call-start = ((), (), s32[]{:S(2)}) async-start(), calls=%async_computation.20 | async-start | bytes 5640192 | tf_op jit(solution)/shard_map/reduce_scatter | solution.py:292
  552.3 242.3 %reduce-scatter.27.cloned.1.call-start = ((), (), s32[]{:S(2)}) async-start(), calls=%async_computation.23 | async-start | bytes 1566720
  662.8 167.6 %reduce-scatter.19.cloned.1.call-start = ((), (), s32[]{:S(2)}) async-start(), calls=%async_computation.19 | async-start | bytes 3538944 | tf_op jit(solution)/shard_map/reduce_scatter | solution.py:250
  680.3 187.1 %reduce-scatter.15.cloned.1.call-start = ((), (), s32[]{:S(2)}) async-start(), calls=%async_computation.15 | async-start | bytes 3538944 | tf_op jit(solution)/shard_map/reduce_scatter | solution.py:190
  694.9 278.8 %reduce-scatter.25.cloned.1.call-start = ((), (), s32[]{:S(2)}) async-start(), calls=%async_computation.22 | async-start | bytes 4386816
  (83 other events, 2793.0 us)
Sparse Core Ops, SparseCore 0:
  10.2 124.2 all-gather.10
  136.6 49.9 all-gather.14
  188.7 34.5 all-gather.12
  225.3 39.3 all-gather.16
  277.8 34.7 reduce-scatter.12
  318.5 36.0 all-gather.18
  357.0 60.6 all-gather.20
  419.9 39.4 all-gather.22
  487.1 34.6 reduce-scatter.16
  530.1 36.0 all-gather.24
  570.2 79.8 reduce-scatter.22
  654.0 78.4 reduce-scatter.20
  736.7 57.8 reduce-scatter.26
  796.8 33.6 reduce-scatter.18
  832.6 34.6 reduce-scatter.14
  871.1 73.1 reduce-scatter.24
